TPU v7x, 256 devices: a whole 4x4x8 slice. The times are simulated.
256 devices in a mesh: sub: 32 (over z_hi, y, core), grp: 8 (over z_lo, x).
Axes of the slice: x: 4, y: 4, z: 8 (z_hi: 4, z_lo: 2; z = z_hi * 2 + z_lo), core: 2. Of those that a mesh axis runs over, the one named last changes fastest.
Arguments:
- right_side: float32 [8, 32, 1024, 128], P('grp', 'sub'), may hold values from -13 to 13
- schur_blocks: bfloat16 [8, 32, 2048, 2048], P('grp', 'sub'), may hold values from -2 to 7, as said below
- occupancy: int32 [8, 32, 1024], P('grp', 'sub'), may hold values 0 or 1
- precond_weights: float32 [8, 32, 1024], P('grp', 'sub'), may hold values from 0.1 to 1
- coarse_basis: float32 [8, 32, 8, 1024], P('grp', 'sub'), may hold values from -0.1875 to 0.1875
- coarse_inverse: float32 [8, 256, 256], P('grp', 'sub'), may hold values from -1 to 5, as said below
Outputs:
- solution: float32 [8, 32, 1024, 128], P('grp', 'sub')
- residual: float32 [8, 32, 1024, 128], P('grp', 'sub')
Inputs may be any that keep to these rules, and one draw needn't show every extreme that they name: `schur_blocks`: each strip's block is symmetric positive definite, diagonal entries between 1.4 and 6.1. `coarse_inverse`: each group's matrix is symmetric positive definite, diagonal entries between 0.9 and 4.2.
All inputs are finite; a program needn't handle non-finite values. No bound on the sum of `occupancy` on one device may be relied on, other than what follows from the above.
Results may differ from a plain program's by a relative error of at most 0.035.
Values may be sent and summed in bfloat16 or wider, within the bound.
A program may use at most 64 MiB of HBM per device.

v0:
```python
import jax
import jax.numpy as jnp
from jax import lax
from jax.sharding import PartitionSpec as P

ITERS = 3


def passed_along(block, axis, distance):
    devices = range(lax.axis_size(axis))
    route = [((i - distance) % len(devices), i) for i in devices]
    return lax.ppermute(block, axis, route)


def shifted(value, axis, steps):
    count = lax.axis_size(axis)
    initial, last = (max(0, -steps), min(count, count - steps))
    return lax.ppermute(value, axis, [(source, source + steps) for source in range(initial, last)])


def local(right_side, schur_blocks, occupancy, precond_weights, coarse_basis, coarse_inverse):
    schur_block = schur_blocks[0, 0]
    free_cells = occupancy[0, 0].astype(jnp.float32)[:, None]
    weight_col = precond_weights[0, 0][:, None]
    basis_rows = coarse_basis[0, 0]
    inverse_rows = coarse_inverse[0]
    source = right_side[0, 0]
    face_cells = source.shape[0]
    group_count = lax.axis_size("sub")
    position = lax.axis_index("sub")
    contract = (((0,), (0,)), ((), ()))

    def precondition(residual):
        coarse = jnp.dot(basis_rows, residual, precision=lax.Precision.HIGHEST)
        group_coarse = lax.all_gather(coarse, "sub", axis=0, tiled=True)
        solved = jnp.dot(inverse_rows, group_coarse, precision=lax.Precision.HIGHEST)
        spread_back = lax.dot_general(basis_rows, solved, contract, precision=lax.Precision.HIGHEST)
        return weight_col * residual + spread_back

    def precond_inner(residual, precond):
        return lax.psum(jnp.sum(residual * precond, axis=0), ("sub", "grp"))

    solution = jnp.zeros_like(source)
    residual = source
    precond = precondition(residual)
    direction = precond
    inner_now = precond_inner(residual, precond)
    for iteration in range(ITERS):
        masked = (free_cells * direction).astype(jnp.bfloat16)
        beside_all = passed_along(masked, "sub", -1)
        crossed = shifted(beside_all, "grp", -1)
        following = jnp.where(position == group_count - 1, crossed, beside_all)
        stacked = jnp.concatenate([masked, following], axis=0)
        product = jnp.dot(schur_block, stacked, preferred_element_type=jnp.float32)
        outgoing = product[face_cells:].astype(jnp.bfloat16)
        behind = passed_along(outgoing, "sub", 1)
        crossed_back = shifted(behind, "grp", 1)
        incoming = jnp.where(position == 0, crossed_back, behind)
        image = (
            free_cells * (product[:face_cells] + incoming.astype(jnp.float32))
            + (1.0 - free_cells) * direction
        )
        step_size = inner_now / lax.psum(jnp.sum(direction * image, axis=0), ("sub", "grp"))
        solution = solution + step_size * direction
        residual = residual - step_size * image
        if iteration + 1 < ITERS:
            precond = precondition(residual)
            inner_next = precond_inner(residual, precond)
            direction = precond + inner_next / inner_now * direction
            inner_now = inner_next
    return (solution[None, None], residual[None, None])


def solution(mesh):
    return jax.shard_map(
        local,
        mesh=mesh,
        in_specs=(
            P("grp", "sub", None, None),
            P("grp", "sub", None, None),
            P("grp", "sub", None),
            P("grp", "sub", None),
            P("grp", "sub", None, None),
            P("grp", "sub", None),
        ),
        out_specs=(P("grp", "sub", None, None), P("grp", "sub", None, None)),
        check_vma=False,
    )
```

profile of v0, /device:TPU:2, one launch (start us, length us, event | category | flops | bytes accessed | tf_op | source)
XLA Modules:
  0.0 647.6 jit_solution(17180566580435164239)
XLA Ops:
  4.0 47.9 %all_gather.9 = f32[256,128]{1,0:T(8,128)S(1)} all-gather(f32[8,128]{1,0:T(8,128)S(1)} %fusion.33), channel_id=1, replica_groups=mesh['sub'=32,'grp'=8] {'sub'}, dimensions={0}, use_global_device_ids=true | all-gather | bytes 135168 | tf_op jit(solution)/shard_map/all_gather | solution.py:35
  54.4 6.7 %collective-permute-done = bf16[1024,128]{0,1:T(8,128)(2,1)S(1)} collective-permute-done((bf16[1024,128]{0,1:T(8,128)(2,1)S(1)}, bf16[1024,128]{0,1:T(8,128)(2,1)S(1)}, u32[]{:S(2)}, u32[]{:S(2)}) %collective-permute-start) | collective-permute-done | bytes 262176 | tf_op jit(solution)/shard_map/ppermute | solution.py:12
  63.5 7.1 %collective-permute-done.1 = bf16[1024,128]{0,1:T(8,128)(2,1)S(1)} collective-permute-done((bf16[1024,128]{0,1:T(8,128)(2,1)S(1)}, bf16[1024,128]{0,1:T(8,128)(2,1)S(1)}, u32[]{:S(2)}, u32[]{:S(2)}) %collective-permute-start.1) | collective-permute-done | bytes 262176 | tf_op jit(solution)/shard_map/ppermute | solution.py:18
  70.6 6.3 fusion.6
  77.0 10.0 %collective-permute-done.2 = bf16[1024,128]{0,1:T(8,128)(2,1)S(1)} collective-permute-done((bf16[1024,128]{0,1:T(8,128)(2,1)S(1)}, bf16[1024,128]{0,1:T(8,128)(2,1)S(1)}, u32[]{:S(2)}, u32[]{:S(2)}) %collective-permute-start.2) | collective-permute-done | bytes 262176 | tf_op jit(solution)/shard_map/ppermute | solution.py:12
  90.4 4.8 collective-permute-done.3
  95.5 76.7 %all-reduce = (f32[128]{0:T(128)S(1)}, f32[128]{0:T(128)S(1)}) all-reduce(f32[128]{0:T(128)S(1)} %get-tuple-element.7, f32[128]{0:T(128)S(1)} %get-tuple-element.6), channel_id=1, replica_groups=mesh['sub'=32,'grp'=8] {'sub','grp'}, use_global_device_ids=true, to_apply=%region_1.0 | all-reduce | flops 256 | bytes 2048 | tf_op jit(solution)/shard_map/psum | solution.py:41
  172.9 40.4 %all_gather.10 = f32[256,128]{1,0:T(8,128)S(1)} all-gather(f32[8,128]{1,0:T(8,128)S(1)} %convolution_bitcast_fusion.4), channel_id=1, replica_groups=mesh['sub'=32,'grp'=8] {'sub'}, dimensions={0}, use_global_device_ids=true | all-gather | bytes 135168 | tf_op jit(solution)/shard_map/all_gather | solution.py:35
  214.4 73.8 %psum.44 = f32[128]{0:T(128)S(1)} all-reduce(f32[128]{0:T(128)S(1)} %get-tuple-element.18), channel_id=1, replica_groups=mesh['sub'=32,'grp'=8] {'sub','grp'}, use_global_device_ids=true, to_apply=%region_5.6 | all-reduce | flops 128 | bytes 1024 | tf_op jit(solution)/shard_map/psum | solution.py:41
  289.8 4.0 collective-permute-done.4
  293.8 4.2 collective-permute-start.5
  298.0 6.2 collective-permute-done.5
  304.3 6.3 fusion.9
  310.8 12.8 %collective-permute-done.6 = bf16[1024,128]{0,1:T(8,128)(2,1)S(1)} collective-permute-done((bf16[1024,128]{0,1:T(8,128)(2,1)S(1)}, bf16[1024,128]{0,1:T(8,128)(2,1)S(1)}, u32[]{:S(2)}, u32[]{:S(2)}) %collective-permute-start.6) | collective-permute-done | bytes 262176 | tf_op jit(solution)/shard_map/ppermute | solution.py:12
  326.4 5.5 collective-permute-done.7
  332.1 73.9 %psum.45 = f32[128]{0:T(128)S(1)} all-reduce(f32[128]{0:T(128)S(1)} %multiply_reduce_fusion.2), channel_id=1, replica_groups=mesh['sub'=32,'grp'=8] {'sub','grp'}, use_global_device_ids=true, to_apply=%region_7.8 | all-reduce | flops 128 | bytes 1024 | tf_op jit(solution)/shard_map/psum | solution.py:63
  407.7 39.3 %all_gather.11 = f32[256,128]{1,0:T(8,128)S(1)} all-gather(f32[8,128]{1,0:T(8,128)S(1)} %convolution_bitcast_fusion.3), channel_id=1, replica_groups=mesh['sub'=32,'grp'=8] {'sub'}, dimensions={0}, use_global_device_ids=true | all-gather | bytes 135168 | tf_op jit(solution)/shard_map/all_gather | solution.py:35
  448.1 73.8 %psum.46 = f32[128]{0:T(128)S(1)} all-reduce(f32[128]{0:T(128)S(1)} %get-tuple-element.20), channel_id=1, replica_groups=mesh['sub'=32,'grp'=8] {'sub','grp'}, use_global_device_ids=true, to_apply=%region_9.10 | all-reduce | flops 128 | bytes 1024 | tf_op jit(solution)/shard_map/psum | solution.py:41
  524.6 4.0 collective-permute-done.8
  531.4 6.5 collective-permute-done.9
  537.9 6.3 fusion.12
  544.3 12.8 %collective-permute-done.10 = bf16[1024,128]{0,1:T(8,128)(2,1)S(1)} collective-permute-done((bf16[1024,128]{0,1:T(8,128)(2,1)S(1)}, bf16[1024,128]{0,1:T(8,128)(2,1)S(1)}, u32[]{:S(2)}, u32[]{:S(2)}) %collective-permute-start.10) | collective-permute-done | bytes 262176 | tf_op jit(solution)/shard_map/ppermute | solution.py:12
  559.1 6.3 collective-permute-done.11
  566.3 75.0 %psum.47 = f32[128]{0:T(128)S(1)} all-reduce(f32[128]{0:T(128)S(1)} %multiply_reduce_fusion), channel_id=1, replica_groups=mesh['sub'=32,'grp'=8] {'sub','grp'}, use_global_device_ids=true, to_apply=%region_11.12 | all-reduce | flops 128 | bytes 1024 | tf_op jit(solution)/shard_map/psum | solution.py:63
  (54 shorter events, 36.1 us)
Async XLA Ops:
  0.6 2.0 copy-start
  54.2 159.1 %copy-start.3 = (f32[1,8,256]{2,1,0:T(8,128)S(1)}, f32[1,8,256]{2,1,0:T(8,128)}, u32[]{:S(2)}) copy-start(f32[1,8,256]{2,1,0:T(8,128)} %param.11) | copy-start | bytes 24580
  54.3 6.8 %collective-permute-start = (bf16[1024,128]{0,1:T(8,128)(2,1)S(1)}, bf16[1024,128]{0,1:T(8,128)(2,1)S(1)}, u32[]{:S(2)}, u32[]{:S(2)}) collective-permute-start(bf16[1024,128]{0,1:T(8,128)(2,1)S(1)} %get-tuple-element.16), channel_id=1, source_target_pairs={{8,0},{16,8},{24,16},{32,24},{40,32},{48,40},{56,48},{64,56},{72,6... | collective-permute-start | bytes 786440 | tf_op jit(solution)/shard_map/ppermute | solution.py:12
  61.0 9.5 %collective-permute-start.1 = (bf16[1024,128]{0,1:T(8,128)(2,1)S(1)}, bf16[1024,128]{0,1:T(8,128)(2,1)S(1)}, u32[]{:S(2)}, u32[]{:S(2)}) collective-permute-start(bf16[1024,128]{0,1:T(8,128)(2,1)S(1)} %collective-permute-done), channel_id=1, source_target_pairs={{1,0},{2,1},{3,2},{4,3},{5,4},{6,5},{7,6},{9,8},{10,9},{11,10},{12... | collective-permute-start | bytes 786440 | tf_op jit(solution)/shard_map/ppermute | solution.py:18
  63.5 150.3 %copy-start.4 = (f32[1,1,1024]{2,1,0:T(1,128)S(1)}, f32[1,1,1024]{2,1,0:T(1,128)}, u32[]{:S(2)}) copy-start(f32[1,1,1024]{2,1,0:T(1,128)} %param.9) | copy-start | bytes 12292
  76.9 10.1 %collective-permute-start.2 = (bf16[1024,128]{0,1:T(8,128)(2,1)S(1)}, bf16[1024,128]{0,1:T(8,128)(2,1)S(1)}, u32[]{:S(2)}, u32[]{:S(2)}) collective-permute-start(bf16[1024,128]{0,1:T(8,128)(2,1)S(1)} %slice.65), channel_id=1, source_target_pairs={{248,0},{0,8},{8,16},{16,24},{24,32},{32,40},{40,48},{48,56},{56,6... | collective-permute-start | bytes 786440 | tf_op jit(solution)/shard_map/ppermute | solution.py:12
  87.0 8.3 %collective-permute-start.3 = (bf16[1024,128]{0,1:T(8,128)(2,1)S(1)}, bf16[1024,128]{0,1:T(8,128)(2,1)S(1)}, u32[]{:S(2)}, u32[]{:S(2)}) collective-permute-start(bf16[1024,128]{0,1:T(8,128)(2,1)S(1)} %collective-permute-done.2), channel_id=1, source_target_pairs={{0,1},{1,2},{2,3},{3,4},{4,5},{5,6},{6,7},{8,9},{9,10},{10,11},{11... | collective-permute-start | bytes 786440 | tf_op jit(solution)/shard_map/ppermute | solution.py:18
  288.4 5.4 collective-permute-start.4
  293.8 10.4 %collective-permute-start.5 = (bf16[1024,128]{0,1:T(8,128)(2,1)S(1)}, bf16[1024,128]{0,1:T(8,128)(2,1)S(1)}, u32[]{:S(2)}, u32[]{:S(2)}) collective-permute-start(bf16[1024,128]{0,1:T(8,128)(2,1)S(1)} %collective-permute-done.4), channel_id=1, source_target_pairs={{1,0},{2,1},{3,2},{4,3},{5,4},{6,5},{7,6},{9,8},{10,9},{11,10},{12... | collective-permute-start | bytes 786440 | tf_op jit(solution)/shard_map/ppermute | solution.py:18
  310.6 13.1 %collective-permute-start.6 = (bf16[1024,128]{0,1:T(8,128)(2,1)S(1)}, bf16[1024,128]{0,1:T(8,128)(2,1)S(1)}, u32[]{:S(2)}, u32[]{:S(2)}) collective-permute-start(bf16[1024,128]{0,1:T(8,128)(2,1)S(1)} %slice.64), channel_id=1, source_target_pairs={{248,0},{0,8},{8,16},{16,24},{24,32},{32,40},{40,48},{48,56},{56,6... | collective-permute-start | bytes 786440 | tf_op jit(solution)/shard_map/ppermute | solution.py:12
  323.6 8.3 %collective-permute-start.7 = (bf16[1024,128]{0,1:T(8,128)(2,1)S(1)}, bf16[1024,128]{0,1:T(8,128)(2,1)S(1)}, u32[]{:S(2)}, u32[]{:S(2)}) collective-permute-start(bf16[1024,128]{0,1:T(8,128)(2,1)S(1)} %collective-permute-done.6), channel_id=1, source_target_pairs={{0,1},{1,2},{2,3},{3,4},{4,5},{5,6},{6,7},{8,9},{9,10},{10,11},{11... | collective-permute-start | bytes 786440 | tf_op jit(solution)/shard_map/ppermute | solution.py:18
  331.9 74.2 %copy-start.1 = (bf16[1024,128]{0,1:T(8,128)(2,1)}, bf16[1024,128]{0,1:T(8,128)(2,1)S(1)}, u32[]{:S(2)}) copy-start(bf16[1024,128]{0,1:T(8,128)(2,1)S(1)} %collective-permute-done.7) | copy-start | bytes 786436
  522.1 6.5 %collective-permute-start.8 = (bf16[1024,128]{0,1:T(8,128)(2,1)S(1)}, bf16[1024,128]{0,1:T(8,128)(2,1)S(1)}, u32[]{:S(2)}, u32[]{:S(2)}) collective-permute-start(bf16[1024,128]{0,1:T(8,128)(2,1)S(1)} %get-tuple-element.10), channel_id=1, source_target_pairs={{8,0},{16,8},{24,16},{32,24},{40,32},{48,40},{56,48},{64,56},{72,6... | collective-permute-start | bytes 786440 | tf_op jit(solution)/shard_map/ppermute | solution.py:12
  528.6 9.3 %collective-permute-start.9 = (bf16[1024,128]{0,1:T(8,128)(2,1)S(1)}, bf16[1024,128]{0,1:T(8,128)(2,1)S(1)}, u32[]{:S(2)}, u32[]{:S(2)}) collective-permute-start(bf16[1024,128]{0,1:T(8,128)(2,1)S(1)} %collective-permute-done.8), channel_id=1, source_target_pairs={{1,0},{2,1},{3,2},{4,3},{5,4},{6,5},{7,6},{9,8},{10,9},{11,10},{12... | collective-permute-start | bytes 786440 | tf_op jit(solution)/shard_map/ppermute | solution.py:18
  544.2 12.9 %collective-permute-start.10 = (bf16[1024,128]{0,1:T(8,128)(2,1)S(1)}, bf16[1024,128]{0,1:T(8,128)(2,1)S(1)}, u32[]{:S(2)}, u32[]{:S(2)}) collective-permute-start(bf16[1024,128]{0,1:T(8,128)(2,1)S(1)} %slice.63), channel_id=1, source_target_pairs={{248,0},{0,8},{8,16},{16,24},{24,32},{32,40},{40,48},{48,56},{56,6... | collective-permute-start | bytes 786440 | tf_op jit(solution)/shard_map/ppermute | solution.py:12
  557.1 8.3 %collective-permute-start.11 = (bf16[1024,128]{0,1:T(8,128)(2,1)S(1)}, bf16[1024,128]{0,1:T(8,128)(2,1)S(1)}, u32[]{:S(2)}, u32[]{:S(2)}) collective-permute-start(bf16[1024,128]{0,1:T(8,128)(2,1)S(1)} %collective-permute-done.10), channel_id=1, source_target_pairs={{0,1},{1,2},{2,3},{3,4},{4,5},{5,6},{6,7},{8,9},{9,10},{10,11},{11... | collective-permute-start | bytes 786440 | tf_op jit(solution)/shard_map/ppermute | solution.py:18
  565.4 0.7 copy-start.2
where the time goes:
time: 649 us; the launch traced here: 648 us
  blocking collectives  501 us (77%)
  waiting for transfers between devices  86.7 us (13%)
  matrix products  25.7 us (4%)
  starting transfers between devices  21.9 us (3%)
    psum x3, blocking collectives, precond_inner(): return lax.psum(jnp.sum(residual * precond, axis=0), ('sub', 'grp'))  224 us
    psum x2, blocking collectives, local(): lax.psum(jnp.sum(direction * image, axis=0), ('sub', 'grp'))  149 us
    all_gather x3, blocking collectives, precondition(): group_coarse = lax.all_gather(coarse, 'sub', axis=0, tiled=True)  128 us
    ppermute x6, waiting for transfers between devices, passed_along(): return lax.ppermute(block, axis, route)  50.4 us
    ppermute x6, waiting for transfers between devices, shifted(): lax.ppermute(value, axis, [(source, source + steps) for source in range(i...  36.4 us
    dot_general x3, matrix products, local(): product = jnp.dot(schur_block, stacked, preferred_element_type=jnp.float32)  18.8 us
    ppermute x6, starting transfers between devices, shifted(): lax.ppermute(value, axis, [(source, source + steps) for source in range(i...  17.5 us
  transfers between devices with their start and end apart: 12, of which 12 were waited for; matrix products, arithmetic and copies ran while one was open for 0% of the time, Pallas kernels for 0%

commit v1 on v0

--- a/solution.py
+++ b/solution.py
@@ -60,7 +60,9 @@
             free_cells * (product[:face_cells] + incoming.astype(jnp.float32))
             + (1.0 - free_cells) * direction
         )
-        step_size = inner_now / lax.psum(jnp.sum(direction * image, axis=0), ("sub", "grp"))
+        step_size = inner_now / jnp.sum(
+            lax.all_gather(jnp.sum(direction * image, axis=0), ("sub", "grp")), axis=0
+        )
         solution = solution + step_size * direction
         residual = residual - step_size * image
         if iteration + 1 < ITERS:

time: 649 us -> 2370 us (3.65)
  blocking collectives: 501 us -> 2220 us
    all_gather x0 -> x3, blocking collectives: none -> 1870 us  [local(): lax.all_gather(jnp.sum(direction * image, axis=0), ('sub', 'grp'))]
    psum x2 -> x0, blocking collectives: 149 us -> none  [local(): lax.psum(jnp.sum(direction * image, axis=0), ('sub', 'grp'))]
where the time goes in v1:
time: 2370 us
  blocking collectives  2220 us (94%)
  waiting for transfers between devices  86 us (4%)
  matrix products  25.7 us (1%)
    all_gather x3, blocking collectives, local(): lax.all_gather(jnp.sum(direction * image, axis=0), ('sub', 'grp'))  1870 us
    psum x3, blocking collectives, precond_inner(): return lax.psum(jnp.sum(residual * precond, axis=0), ('sub', 'grp'))  225 us
    all_gather x3, blocking collectives, precondition(): group_coarse = lax.all_gather(coarse, 'sub', axis=0, tiled=True)  126 us
    ppermute x6, waiting for transfers between devices, passed_along(): return lax.ppermute(block, axis, route)  50.4 us
  transfers between devices with their start and end apart: 12, of which 12 were waited for; matrix products, arithmetic and copies ran while one was open for 0% of the time, Pallas kernels for 0%

profile of v1, /device:TPU:2, one launch (start us, length us, event | category | flops | bytes accessed | tf_op | source)
XLA Modules:
  0.0 2369.4 jit_solution(9957530745096427557)
XLA Ops:
  4.0 47.9 %all_gather.27 = f32[256,128]{1,0:T(8,128)S(1)} all-gather(f32[8,128]{1,0:T(8,128)S(1)} %fusion.33), channel_id=1, replica_groups=mesh['sub'=32,'grp'=8] {'sub'}, dimensions={0}, use_global_device_ids=true | all-gather | bytes 135168 | tf_op jit(solution)/shard_map/all_gather | solution.py:35
  54.3 6.7 collective-permute-done
  63.5 7.1 collective-permute-done.1
  70.6 6.3 fusion.6
  77.0 10.0 collective-permute-done.2
  90.4 4.8 collective-permute-done.3
  95.5 76.7 %psum.21 = f32[128]{0:T(128)S(1)} all-reduce(f32[128]{0:T(128)S(1)} %get-tuple-element.7), channel_id=1, replica_groups=mesh['sub'=32,'grp'=8] {'sub','grp'}, use_global_device_ids=true, to_apply=%region_1.0 | all-reduce | flops 128 | bytes 1024 | tf_op jit(solution)/shard_map/psum | solution.py:41
  172.3 617.0 %all-gather.3 = f32[256,1,128]{2,1,0:T(1,128)S(1)} all-gather(f32[1,1,128]{2,1,0:T(1,128)S(1)} %bitcast.102), channel_id=2, replica_groups=mesh['sub'=32,'grp'=8] {'sub','grp'}, dimensions={0}, use_global_device_ids=true | all-gather | bytes 131584 | tf_op jit(solution)/shard_map/all_gather | solution.py:64
  790.2 39.2 %all_gather.30 = f32[256,128]{1,0:T(8,128)S(1)} all-gather(f32[8,128]{1,0:T(8,128)S(1)} %convolution_bitcast_fusion.4), channel_id=1, replica_groups=mesh['sub'=32,'grp'=8] {'sub'}, dimensions={0}, use_global_device_ids=true | all-gather | bytes 135168 | tf_op jit(solution)/shard_map/all_gather | solution.py:35
  830.5 74.1 %psum.22 = f32[128]{0:T(128)S(1)} all-reduce(f32[128]{0:T(128)S(1)} %get-tuple-element.16), channel_id=1, replica_groups=mesh['sub'=32,'grp'=8] {'sub','grp'}, use_global_device_ids=true, to_apply=%region_5.6 | all-reduce | flops 128 | bytes 1024 | tf_op jit(solution)/shard_map/psum | solution.py:41
  906.3 4.0 collective-permute-done.4
  914.3 6.3 collective-permute-done.5
  920.6 6.3 fusion.9
  927.0 12.8 collective-permute-done.6
  942.6 5.5 collective-permute-done.7
  948.3 615.9 %all-gather.4 = f32[256,1,128]{2,1,0:T(1,128)S(1)} all-gather(f32[1,1,128]{2,1,0:T(1,128)S(1)} %bitcast.103), channel_id=3, replica_groups=mesh['sub'=32,'grp'=8] {'sub','grp'}, dimensions={0}, use_global_device_ids=true | all-gather | bytes 131584 | tf_op jit(solution)/shard_map/all_gather | solution.py:64
  1566.1 39.2 %all_gather.33 = f32[256,128]{1,0:T(8,128)S(1)} all-gather(f32[8,128]{1,0:T(8,128)S(1)} %convolution_bitcast_fusion.3), channel_id=1, replica_groups=mesh['sub'=32,'grp'=8] {'sub'}, dimensions={0}, use_global_device_ids=true | all-gather | bytes 135168 | tf_op jit(solution)/shard_map/all_gather | solution.py:35
  1606.3 74.2 %psum.23 = f32[128]{0:T(128)S(1)} all-reduce(f32[128]{0:T(128)S(1)} %get-tuple-element.18), channel_id=1, replica_groups=mesh['sub'=32,'grp'=8] {'sub','grp'}, use_global_device_ids=true, to_apply=%region_9.10 | all-reduce | flops 128 | bytes 1024 | tf_op jit(solution)/shard_map/psum | solution.py:41
  1682.2 4.0 collective-permute-done.8
  1690.1 6.5 collective-permute-done.9
  1696.6 6.3 fusion.12
  1703.0 12.9 collective-permute-done.10
  1718.7 5.5 collective-permute-done.11
  1725.0 636.9 %all-gather.5 = f32[256,1,128]{2,1,0:T(1,128)} all-gather(f32[1,1,128]{2,1,0:T(1,128)S(1)} %bitcast.104), channel_id=4, replica_groups=mesh['sub'=32,'grp'=8] {'sub','grp'}, dimensions={0}, use_global_device_ids=true | all-gather | bytes 131584 | tf_op jit(solution)/shard_map/all_gather | solution.py:64
  (58 shorter events, 42.7 us)
Async XLA Ops:
  0.6 2.0 copy-start
  54.2 6.8 collective-permute-start
  61.0 9.5 collective-permute-start.1
  63.5 765.9 %copy-start.3 = (f32[1,8,256]{2,1,0:T(8,128)S(1)}, f32[1,8,256]{2,1,0:T(8,128)}, u32[]{:S(2)}) copy-start(f32[1,8,256]{2,1,0:T(8,128)} %param.11) | copy-start | bytes 24580
  70.6 759.2 %copy-start.4 = (f32[1,1,1024]{2,1,0:T(1,128)S(1)}, f32[1,1,1024]{2,1,0:T(1,128)}, u32[]{:S(2)}) copy-start(f32[1,1,1024]{2,1,0:T(1,128)} %param.9) | copy-start | bytes 12292
  76.9 10.1 collective-permute-start.2
  87.0 8.3 collective-permute-start.3
  904.7 5.5 collective-permute-start.4
  910.3 10.3 collective-permute-start.5
  926.9 12.9 collective-permute-start.6
  939.8 8.3 collective-permute-start.7
  948.0 616.4 %copy-start.1 = (bf16[1024,128]{0,1:T(8,128)(2,1)}, bf16[1024,128]{0,1:T(8,128)(2,1)S(1)}, u32[]{:S(2)}) copy-start(bf16[1024,128]{0,1:T(8,128)(2,1)S(1)} %collective-permute-done.7) | copy-start | bytes 786436
  1680.7 5.5 collective-permute-start.8
  1686.3 10.3 collective-permute-start.9
  1702.9 13.0 collective-permute-start.10
  1715.9 8.3 collective-permute-start.11
  1724.1 0.7 copy-start.2
